TPU v7x, 32 devices: a whole 2x2x4 slice. The times are simulated.
32 devices in a mesh: ctx: 8 (over y, x, core), tp: 4 (over z).
Axes of the slice: x: 2, y: 2, z: 4, core: 2. Of those that a mesh axis runs over, the one named last changes fastest.
Arguments:
- queries: bfloat16 [2048, 4096], P('ctx', 'tp'), may hold values from -100 to 100
- key_pages: bfloat16 [32, 64, 1024], P('ctx', None, 'tp'), may hold values from -5 to 5
- value_pages: bfloat16 [32, 64, 1024], P('ctx', None, 'tp'), may hold values from -6 to 6
- mixer_input: bfloat16 [2048, 4096], P('ctx', 'tp'), may hold values from -6 to 6
- state_write: bfloat16 [2048, 1024], P('ctx', 'tp'), may hold values from -0.029907227 to 0.029907227
- state_read: bfloat16 [2048, 1024], P('ctx', 'tp'), may hold values from -6 to 6
- log_decay: float32 [32, 2048], P('tp', 'ctx'), may hold values from -1 to 0
- skip_gain: float32 [32], P('tp'), may hold values from 0.5 to 1.5
- doc_lengths: int32 [4], replicated, may hold values from 1 to 1024, 2048 in all
- page_table: int32 [32], replicated, may hold values from 0 to 31, as said below
- attention_weight: bfloat16 [4096, 4096], P('tp'), may hold values from -0.75 to 0.75
- mixer_weight: bfloat16 [4096, 4096], P('tp'), may hold values from -0.09375 to 0.09375
Outputs:
- mixed: bfloat16 [2048, 4096], P(('ctx', 'tp'))
Inputs may be any that keep to these rules, and one draw needn't show every extreme that they name: `doc_lengths`: the lengths sum to 2048; the longest is exactly 1024. `page_table`: A permutation: every physical page holds exactly one logical page.
All inputs are finite; a program needn't handle non-finite values.
Results may differ from a plain program's by a relative error of at most 0.007.
Values may be sent and summed in bfloat16 or wider, within the bound.
No kernel may reach another device: no remote copies, remote signals or barrier semaphores. Data moves between devices by JAX's collectives and lax.ppermute only.
A program may use at most 256 MiB of HBM per device.

v0:
```python
import jax
import jax.numpy as jnp
from jax import lax
from jax.sharding import PartitionSpec as P

HEAD_DIM = 128
SSM_HEAD_DIM = 128
STATE = 128


def entering(array, axis, join, neutral):
    place = lax.axis_index(axis)
    gathered = jax.tree.map(
        lambda a, kind: lax.all_gather(a.astype(kind), axis), array, (jnp.bfloat16, jnp.bfloat16)
    )
    state = jax.tree.map(lambda a, e: jnp.zeros_like(a) + jnp.asarray(e, a.dtype), array, neutral)

    def one(lap, state):
        return join(
            state,
            jax.tree.map(
                lambda a, own: lax.dynamic_index_in_dim(a, lap, 0, False).astype(own.dtype),
                gathered,
                array,
            ),
        )

    return lax.fori_loop(0, place, one, state)


def segment_of(positions, doc_ends):
    return jnp.sum((positions[:, None] >= doc_ends[None, :]).astype(jnp.int32), axis=1)


def mixer_local(head_input, write_rows, read_rows, decay_rows, block_seg, prev_seg, per_group):
    tok_rows = head_input.shape[0]
    decay_sum = jnp.cumsum(decay_rows, axis=1)
    token_order = jnp.arange(tok_rows, dtype=jnp.int32)
    visible = (token_order[None, :] <= token_order[:, None]) & (
        block_seg[None, :] == block_seg[:, None]
    )
    decay_diff = decay_sum[:, :, None] - decay_sum[:, None, :]
    decay_mat = jnp.where(visible[None], jnp.exp(jnp.minimum(decay_diff, 0.0)), 0.0)
    inner_prod = jnp.einsum(
        "tgn,sgn->gts", read_rows, write_rows, preferred_element_type=jnp.float32
    )
    mixing = (decay_mat * jnp.repeat(inner_prod, per_group, axis=0)).astype(jnp.bfloat16)
    intra_out = jnp.einsum("hts,shp->thp", mixing, head_input, preferred_element_type=jnp.float32)
    end_seg = block_seg[-1]
    end_weight = jnp.where(
        (block_seg == end_seg)[None, :], jnp.exp(decay_sum[:, -1:] - decay_sum), 0.0
    )
    write_heads = jnp.repeat(write_rows, per_group, axis=1)
    end_write = (jnp.transpose(end_weight)[:, :, None] * write_heads).astype(jnp.bfloat16)
    block_state = jnp.einsum(
        "thn,thp->hnp", end_write, head_input, preferred_element_type=jnp.float32
    )
    block_gain = jnp.where(end_seg == prev_seg, jnp.exp(decay_sum[:, -1]), 0.0)
    return (intra_out, block_gain, block_state, decay_sum)


def mixer_entry(
    intra_out, decay_sum, read_rows, head_input, skip_gain, block_seg, prev_seg, state_in, per_group
):
    read_heads = jnp.repeat(read_rows, per_group, axis=1).astype(jnp.float32)
    inter_out = jnp.einsum("thn,hnp->thp", read_heads, state_in, precision=lax.Precision.HIGHEST)
    entry_gain = jnp.where((block_seg == prev_seg)[None, :], jnp.exp(decay_sum), 0.0)
    return (
        intra_out
        + jnp.transpose(entry_gain)[:, :, None] * inter_out
        + skip_gain[None, :, None] * head_input.astype(jnp.float32)
    )


def compose_states(earlier, later):
    return (earlier[0] * later[0], later[0][:, None, None] * earlier[1] + later[1])


def shards(
    queries,
    key_pages,
    value_pages,
    mixer_input,
    state_write,
    state_read,
    log_decay,
    skip_gain,
    doc_lengths,
    page_table,
    attention_weight,
    mixer_weight,
):
    my_block = lax.axis_index("ctx")
    tok_rows = queries.shape[0]
    doc_ends = jnp.cumsum(doc_lengths)
    first_pos = my_block * tok_rows
    positions = first_pos + jnp.arange(tok_rows, dtype=jnp.int32)
    query_seg = segment_of(positions, doc_ends)
    head_local = queries.shape[1] // HEAD_DIM
    kv_local = key_pages.shape[2] // HEAD_DIM
    group_size = head_local // kv_local
    page_len = key_pages.shape[1]
    page_total = page_table.shape[0]
    page_ids = jnp.arange(page_total, dtype=jnp.int32)
    logical_of = jnp.sum(
        jnp.where(page_table[:, None] == page_ids[None, :], page_ids[:, None], 0), axis=0
    )
    query_heads = queries.reshape(tok_rows, kv_local, group_size, HEAD_DIM)
    stat_shape = (tok_rows, kv_local, group_size)
    key_rows = lax.all_gather(key_pages, "ctx", axis=0, tiled=True)
    page_count = key_rows.shape[0]
    key_pos = (
        logical_of[:, None] * page_len + jnp.arange(page_len, dtype=jnp.int32)[None, :]
    ).reshape(-1)
    key_seg = segment_of(key_pos, doc_ends)
    visible = (key_pos[None, :] <= positions[:, None]) & (key_seg[None, :] == query_seg[:, None])
    flat_keys = key_rows.reshape(page_count * page_len, kv_local, HEAD_DIM)
    flat_values = lax.all_gather(value_pages, "ctx", axis=0, tiled=True).reshape(
        page_count * page_len, kv_local, HEAD_DIM
    )
    run_max = jnp.full(stat_shape, -1e30, jnp.float32)
    scores = jnp.einsum(
        "tgjd,sgd->tgjs", query_heads, flat_keys, preferred_element_type=jnp.float32
    ) * HEAD_DIM ** (-0.5)
    shown = visible[:, None, None, :]
    new_max = jnp.maximum(run_max, jnp.max(jnp.where(shown, scores, -1e30), axis=3))
    weights = jnp.where(shown, jnp.exp(scores - new_max[..., None]), 0.0)
    new_sum = jnp.sum(weights, axis=3)
    probabilities = weights.astype(jnp.bfloat16)
    new_acc = jnp.einsum(
        "tgjs,sgd->tgjd", probabilities, flat_values, preferred_element_type=jnp.float32
    )
    attention_out = (
        (new_acc / new_sum[..., None]).reshape(tok_rows, head_local * HEAD_DIM).astype(jnp.bfloat16)
    )
    ssm_local = mixer_input.shape[1] // SSM_HEAD_DIM
    group_local = state_write.shape[1] // STATE
    per_group = ssm_local // group_local
    head_input = mixer_input.reshape(tok_rows, ssm_local, SSM_HEAD_DIM)
    write_rows = state_write.reshape(tok_rows, group_local, STATE)
    read_rows = state_read.reshape(tok_rows, group_local, STATE)
    before_pos = jnp.reshape(first_pos - 1, (1,))
    prev_seg = jnp.where(first_pos > 0, segment_of(before_pos, doc_ends)[0], -1)
    intra_out, block_gain, block_state, decay_sum = mixer_local(
        head_input, write_rows, read_rows, log_decay, query_seg, prev_seg, per_group
    )
    gain_in, state_in = entering(
        (block_gain, block_state),
        "ctx",
        compose_states,
        (jnp.ones_like(block_gain), jnp.zeros_like(block_state)),
    )
    mixer_rows = mixer_entry(
        intra_out,
        decay_sum,
        read_rows,
        head_input,
        skip_gain,
        query_seg,
        prev_seg,
        state_in,
        per_group,
    )
    mixer_out = mixer_rows.reshape(tok_rows, ssm_local * SSM_HEAD_DIM).astype(jnp.bfloat16)
    mixed = lax.psum_scatter(
        jnp.dot(attention_out, attention_weight, preferred_element_type=jnp.float32)
        + jnp.dot(mixer_out, mixer_weight, preferred_element_type=jnp.float32),
        "tp",
        scatter_dimension=0,
        tiled=True,
    )
    return mixed.astype(jnp.bfloat16)


def solution(mesh):
    placed = (
        P("ctx", "tp"),
        P("ctx", None, "tp"),
        P("ctx", None, "tp"),
        P("ctx", "tp"),
        P("ctx", "tp"),
        P("ctx", "tp"),
        P("tp", "ctx"),
        P("tp"),
        P(),
        P(),
        P("tp", None),
        P("tp", None),
    )
    return jax.shard_map(
        shards, mesh=mesh, in_specs=placed, out_specs=P(("ctx", "tp"), None), check_vma=False
    )
```

profile of v0, /device:TPU:0, one launch (start us, length us, event | category | flops | bytes accessed | tf_op | source)
XLA Modules:
  0.0 194.3 jit_solution(17334929127929989161)
XLA Ops:
  6.5 0.0 copy-start
  6.5 0.0 copy-start.2
  6.5 0.0 all-gather.6.cloned.1.call-start
  6.5 0.7 all-gather.6.cloned.1.call-update
  7.3 0.0 all-gather.8.cloned.1.call-start
  7.3 0.7 all-gather.8.cloned.1.call-update
  8.0 0.0 all-gather.10.cloned.1.call-start
  8.1 0.8 reduce-window.10
  8.9 0.1 convert_reduce_fusion.1
  9.0 0.6 slice.15
  9.6 1.2 reduce-window.11
  10.8 0.2 slice_reduce_fusion
  11.0 1.2 copy.66
  12.3 0.9 reshape.265
  13.2 0.1 copy.67
  13.3 0.6 fusion.30
  14.6 0.7 broadcast_compare_fusion
  15.3 0.1 select_bitcast_fusion.1
  15.3 0.2 slice_reduce_fusion.1
  15.5 0.1 select_bitcast_fusion
  15.6 0.1 fusion.16
  15.7 1.0 convolution_convert_fusion
  16.7 0.0 all-gather.10.cloned.1.call-update
  16.8 0.0 reduce-scatter.2.cloned.1.call-start
  16.8 0.1 fusion.25
  17.6 0.0 copy-done
  17.6 1.1 fusion.26
  18.7 0.7 select_reduce_fusion
  19.5 0.1 iota_add_fusion
  19.6 0.1 add.64
  19.6 0.1 convert_reduce_fusion
  19.7 1.4 compare_and_fusion
  21.2 2.2 %reshape.260 = bf16[256,2,4,128]{3,2,1,0:T(4,128)(2,1)} reshape(bf16[256,1024]{1,0:T(8,128)(2,1)} %param.14) | data formatting | bytes 1048576 | tf_op jit(solution)/shard_map/reshape | solution.py:108
  23.4 0.5 fusion.8
  23.9 0.5 convolution_bitcast_fusion.1
  24.4 0.2 fusion.29
  24.6 0.0 copy-done.2
  24.6 0.7 dynamic-slice
  26.0 0.2 dynamic-update-slice
  26.2 15.3 %all-reduce = bf16[64]{0:T(256)(128)(2,1)S(1)} all-reduce(bf16[64]{0:T(256)(128)(2,1)S(1)} %dynamic-update-slice), channel_id=2, replica_groups=mesh['ctx'=8,'tp'=4] {'ctx'}, use_global_device_ids=true, to_apply=%add | all-reduce | flops 64 | bytes 256
  41.6 0.1 reshape.271
  41.7 0.0 all-gather.6.cloned.1.call-done
  41.7 1.3 reshape.259
  43.0 8.3 %fusion = (f32[256,2,4]{0,2,1:T(4,128)S(1)}, f32[2,2048,256,4]{2,1,3,0:T(8,128)}) fusion(pred[256,2048]{0,1:T(8,128)(4,1)S(1)} %compare_and_fusion, bf16[256,2,4,128]{3,2,1,0:T(4,128)(2,1)} %reshape.260, bf16[2048,2,128,1]{2,1,0,3:T(2,128)(2,1)S(1)} %bitcast.103), kind=kOutput, calls=%fused_computation.4 | convolution fusion | flops 1086322688 | bytes 18882560 | tf_op jit(solution)/shard_map/tgjd,sgd->tgjs/dot_general | solution.py:122
  51.3 9.7 %all-gather.8.cloned.1.call-done = bf16[32,64,256]{2,1,0:T(8,128)(2,1)} async-done(((bf16[4,64,256]{2,1,0:T(8,128)(2,1)}), bf16[32,64,256]{2,1,0:T(8,128)(2,1)}) %all-gather.8.cloned.1.call-update) | async-done | bytes 1048592 | tf_op jit(solution)/shard_map/all_gather | solution.py:118
  61.0 1.3 reshape.261
  62.4 9.2 %fusion.3 = f32[256,2,4]{0,2,1:T(4,128)S(1)} fusion(f32[2,2048,256,4]{2,1,3,0:T(8,128)} %get-tuple-element.65, f32[256,2,4]{0,2,1:T(4,128)S(1)} %broadcast_maximum_fusion, pred[256,2048]{0,1:T(8,128)(4,1)S(1)} %compare_and_fusion), kind=kLoop, calls=%fused_computation.7 | loop fusion | flops 16775168 | bytes 17317888 | tf_op jit(solution)/shard_map/reduce_sum | solution.py:128
  71.5 7.8 %divide_convert_fusion = bf16[256,2,4,128]{0,3,2,1:T(8,128)(2,1)S(1)} fusion(f32[2,2048,256,4]{2,1,3,0:T(8,128)} %get-tuple-element.65, f32[256,2,4]{0,2,1:T(4,128)S(1)} %broadcast_maximum_fusion, pred[256,2048]{0,1:T(8,128)(4,1)S(1)} %compare_and_fusion, bf16[2048,2,128,1]{2,1,0,3:T(2,128)(2,1)S(1)} %bitcast.102, f32[256,2,4]{0,2,1:T(4,128)S(1)} %fusion.3), kind=kOutput, calls=%fused_computation.28 | convolution fusion | flops 1091043328 | bytes 18890752 | tf_op jit(solution)/shard_map/tgjs,sgd->tgjd/dot_general | solution.py:130
  79.3 0.0 copy-start.1
  79.3 8.0 %fusion.33 = f32[256,4096]{1,0:T(8,128)} fusion(bf16[256,1024]{0,1:T(8,128)(2,1)S(1)} %bitcast.105, bf16[1024,4096]{1,0:T(8,128)(2,1)} %param.24), kind=kOutput, calls=%fused_computation.57 | convolution fusion | flops 2147483648 | bytes 13107200 | tf_op jit(solution)/shard_map/dot_general | solution.py:166
  87.4 3.4 %all-gather.10.cloned.1.call-done = bf16[64,128,128]{2,1,0:T(8,128)(2,1)} async-done(((bf16[8,128,128]{2,1,0:T(8,128)(2,1)}), bf16[64,128,128]{2,1,0:T(8,128)(2,1)}) %all-gather.10.cloned.1.call-update) | async-done | bytes 2097168 | tf_op jit(solution)/shard_map/all_gather | solution.py:14
  90.9 0.2 while.12
  91.1 0.1 broadcast_in_dim.120
  91.2 0.0 copy-done.1
  91.2 0.7 fusion.15
  91.9 8.9 %convolution_add_fusion = f32[256,4096]{1,0:T(8,128)} fusion(f32[256,4096]{1,0:T(8,128)} %fusion.33, bf16[256,1024]{0,1:T(8,128)(2,1)S(1)} %bitcast.101, bf16[1024,4096]{1,0:T(8,128)(2,1)} %param.25), kind=kOutput, calls=%fused_computation.11 | convolution fusion | flops 2148532224 | bytes 17301504 | tf_op jit(solution)/shard_map/dot_general | solution.py:167
  100.8 0.0 reduce-scatter.2.cloned.1.call-update
  100.9 84.8 %reduce-scatter.2.cloned.1.call-done = f32[64,4096]{1,0:T(8,128)} async-done(((f32[256,4096]{1,0:T(8,128)}), f32[64,4096]{1,0:T(8,128)}) %reduce-scatter.2.cloned.1.call-update) | async-done | bytes 1048592 | tf_op jit(solution)/shard_map/reduce_scatter | solution.py:165
  185.7 2.1 %convert_element_type.103 = bf16[64,4096]{1,0:T(8,128)(2,1)} convert(f32[64,4096]{1,0:T(8,128)} %reduce-scatter.2.cloned.1.call-done) | non-fusion elementwise | flops 262144 | bytes 1572864 | tf_op jit(solution)/shard_map/convert_element_type | solution.py:172
  (8 shorter events, 0.1 us)
Async XLA Ops:
  6.5 11.0 %copy-start = (bf16[256,256]{1,0:T(8,128)(2,1)S(1)}, bf16[256,256]{1,0:T(8,128)(2,1)}, u32[]{:S(2)}) copy-start(bf16[256,256]{1,0:T(8,128)(2,1)} %param.19) | copy-start | bytes 393220
  6.5 18.1 %copy-start.2 = (u32[32]{0:T(128)S(1)}, u32[32]{0:T(128)}, u32[]{:S(2)}) copy-start(u32[32]{0:T(128)} %constant.53) | copy-start | bytes 388
  6.5 35.1 %all-gather.6.cloned.1.call-start = ((), (), s32[]{:S(2)}) async-start(), calls=%async_computation.1 | async-start | bytes 1179648 | tf_op jit(solution)/shard_map/all_gather | solution.py:110
  7.3 53.7 %all-gather.8.cloned.1.call-start = ((), (), s32[]{:S(2)}) async-start(), calls=%async_computation.2 | async-start | bytes 1179648 | tf_op jit(solution)/shard_map/all_gather | solution.py:118
  8.0 82.8 %all-gather.10.cloned.1.call-start = ((), (), s32[]{:S(2)}) async-start(), calls=%async_computation.4 | async-start | bytes 2359296 | tf_op jit(solution)/shard_map/all_gather | solution.py:14
  16.8 169.0 %reduce-scatter.2.cloned.1.call-start = ((), (), s32[]{:S(2)}) async-start(), calls=%async_computation.3 | async-start | bytes 5242880 | tf_op jit(solution)/shard_map/reduce_scatter | solution.py:165
  79.3 11.8 %copy-start.1 = (f32[8]{0:T(128)S(1)}, f32[8]{0:T(128)}, u32[]{:S(2)}) copy-start(f32[8]{0:T(128)} %param.21) | copy-start | bytes 100
Sparse Core Ops, SparseCore 0:
  9.2 26.3 all-gather.5
  37.5 23.4 all-gather.7
  62.9 27.8 all-gather.9
  101.0 84.6 reduce-scatter.1
where the time goes:
time: 195 us; the launch traced here: 194 us
  waiting for transfers between devices  99.4 us (51%)
  matrix products  36.4 us (19%)
  other arithmetic  18.2 us (9%)
  blocking collectives  15.3 us (8%)
  between operations  15.3 us (8%)
  local copies, waits for them, and re-layouts  9.32 us (5%)
    reduce_scatter x1, waiting for transfers between devices, shards(): lax.psum_scatter(jnp.dot(attention_out, attention_weight, preferred_eleme...  84.8 us
    unnamed x1, blocking collectives  15.3 us
    all_gather x1, waiting for transfers between devices, shards(): lax.all_gather(value_pages, 'ctx', axis=0, tiled=True)  9.7 us
    reduce_sum x1, other arithmetic, shards(): new_sum = jnp.sum(weights, axis=3)  9.17 us
    dot_general x1, matrix products, shards(): jnp.dot(mixer_out, mixer_weight, preferred_element_type=jnp.float32)  8.91 us
    dot_general x1, matrix products, shards(): jnp.einsum('tgjd,sgd->tgjs', query_heads, flat_keys, preferred_element_ty...  8.3 us
    dot_general x1, matrix products, shards(): jnp.dot(attention_out, attention_weight, preferred_element_type=jnp.float32)  8.04 us
    dot_general x1, matrix products, shards(): jnp.einsum('tgjs,sgd->tgjd', probabilities, flat_values, preferred_elemen...  7.79 us
  transfers between devices with their start and end apart: 4, of which 3 were waited for; matrix products, arithmetic and copies ran while one was open for 27% of the time, Pallas kernels for 0%

commit v1 on v0

--- a/solution.py
+++ b/solution.py
@@ -115,9 +115,34 @@
     key_seg = segment_of(key_pos, doc_ends)
     visible = (key_pos[None, :] <= positions[:, None]) & (key_seg[None, :] == query_seg[:, None])
     flat_keys = key_rows.reshape(page_count * page_len, kv_local, HEAD_DIM)
-    flat_values = lax.all_gather(value_pages, "ctx", axis=0, tiled=True).reshape(
-        page_count * page_len, kv_local, HEAD_DIM
-    )
+
+    def _store_vectors(xx):
+        back = lax.axis_index("ctx")
+        now = lax.axis_size("ctx")
+        latest, r_now, state_now = (now, back, xx.shape[0])
+        runs = [kk * latest if ix == 0 else kk for ix, kk in enumerate(xx.shape)]
+        current_block = jnp.zeros(runs, xx.dtype)
+        arr_now = state_next = xx
+        block_out = lax.dynamic_update_slice_in_dim(current_block, xx, r_now * state_now, axis=0)
+        for hop_no in range(1, latest // 2 + 1):
+            reply = range(latest)
+            last = map(lambda ix: (ix, (ix + 1) % latest), reply)
+            current_value = list(last)
+            arr_now = lax.ppermute(arr_now, "ctx", current_value)
+            block_out = lax.dynamic_update_slice_in_dim(
+                block_out, arr_now, (r_now - hop_no) % latest * state_now, axis=0
+            )
+            if 2 * hop_no < latest:
+                piece_now = range(latest)
+                x_now = map(lambda ix: (ix, (ix - 1) % latest), piece_now)
+                u_next = list(x_now)
+                state_next = lax.ppermute(state_next, "ctx", u_next)
+                block_out = lax.dynamic_update_slice_in_dim(
+                    block_out, state_next, (r_now + hop_no) % latest * state_now, axis=0
+                )
+        return block_out
+
+    flat_values = _store_vectors(value_pages).reshape(page_count * page_len, kv_local, HEAD_DIM)
     run_max = jnp.full(stat_shape, -1e30, jnp.float32)
     scores = jnp.einsum(
         "tgjd,sgd->tgjs", query_heads, flat_keys, preferred_element_type=jnp.float32

time: 195 us -> 197 us (1.010)
  starting transfers between devices: 0.12 us -> 9 us
  waiting for transfers between devices: 99.4 us -> 95 us
  blocking collectives: 15.3 us -> 12.6 us
    ppermute x0 -> x7, waiting for transfers between devices: none -> 11.3 us  [the longest x4 8.3 us: _store_vectors(): arr_now = lax.ppermute(arr_now, 'ctx', current_value)]
    all_gather x1 -> x0, waiting for transfers between devices: 9.7 us -> none  [shards(): lax.all_gather(value_pages, 'ctx', axis=0, tiled=True)]
    ppermute x0 -> x7, starting transfers between devices: none -> 8.89 us  [the longest x3 8.32 us: _store_vectors(): state_next = lax.ppermute(state_next, 'ctx', u_next)]
    all_gather x1, waiting for transfers between devices: 3.44 us -> 0.01 us  [entering(): lax.all_gather(a.astype(kind), axis)]
    unnamed x1, blocking collectives: 15.3 us -> 12.6 us
  transfers between devices with their start and end apart: 4 -> 10, of which waited for: 3 -> 6; matrix products, arithmetic and copies ran while one was open for 27% -> 27% of each run, Pallas kernels for 0% -> 0%
where the time goes in v1:
time: 197 us
  waiting for transfers between devices  95 us (48%)
  matrix products  36 us (18%)
  other arithmetic  18.3 us (9%)
  between operations  15.4 us (8%)
  blocking collectives  12.6 us (6%)
  local copies, waits for them, and re-layouts  10 us (5%)
  starting transfers between devices  9 us (5%)
    reduce_scatter x1, waiting for transfers between devices, shards(): lax.psum_scatter(jnp.dot(attention_out, attention_weight, preferred_eleme...  83 us
    unnamed x1, blocking collectives  12.6 us
    reduce_sum x1, other arithmetic, shards(): new_sum = jnp.sum(weights, axis=3)  9.25 us
    dot_general x1, matrix products, shards(): jnp.dot(mixer_out, mixer_weight, preferred_element_type=jnp.float32)  8.91 us
    dot_general x1, matrix products, shards(): jnp.einsum('tgjd,sgd->tgjs', query_heads, flat_keys, preferred_element_ty...  8.33 us
    ppermute x3, starting transfers between devices, _store_vectors(): state_next = lax.ppermute(state_next, 'ctx', u_next)  8.32 us
    ppermute x4, waiting for transfers between devices, _store_vectors(): arr_now = lax.ppermute(arr_now, 'ctx', current_value)  8.3 us
    dot_general x1, matrix products, shards(): jnp.dot(attention_out, attention_weight, preferred_element_type=jnp.float32)  7.69 us
  transfers between devices with their start and end apart: 10, of which 6 were waited for; matrix products, arithmetic and copies ran while one was open for 27% of the time, Pallas kernels for 0%

profile of v1, /device:TPU:0, one launch (start us, length us, event | category | flops | bytes accessed | tf_op | source)
XLA Modules:
  0.0 196.5 jit_solution(11498557902759186614)
XLA Ops:
  6.5 0.0 all-gather.5.cloned.1.call-start
  6.6 0.7 all-gather.5.cloned.1.call-update
  7.3 0.0 all-gather.7.cloned.1.call-start
  7.3 0.5 collective-permute-start
  7.8 2.9 %collective-permute-start.1 = (bf16[4,64,256]{2,1,0:T(8,128)(2,1)}, bf16[4,64,256]{2,1,0:T(8,128)(2,1)}, u32[]{:S(2)}, u32[]{:S(2)}) collective-permute-start(bf16[4,64,256]{2,1,0:T(8,128)(2,1)} %param.16), channel_id=1, source_target_pairs={{0,28},{4,0},{8,4},{12,8},{16,12},{20,16},{24,20},{28,24},{1,29},{... | collective-permute-start | bytes 393224 | tf_op jit(solution)/shard_map/ppermute | solution.py:139
  10.8 0.8 reduce-window.10
  11.6 0.1 convert_reduce_fusion.1
  11.7 0.6 slice.15
  12.3 1.2 reduce-window.11
  13.5 0.2 slice_reduce_fusion
  13.7 1.2 copy.73
  15.0 0.9 reshape.265
  15.9 0.1 copy.74
  16.0 0.6 fusion.30
  17.3 0.7 broadcast_compare_fusion
  18.0 0.1 select_bitcast_fusion.1
  18.0 0.2 slice_reduce_fusion.1
  18.2 0.1 select_bitcast_fusion
  18.3 0.1 fusion.16
  18.4 1.0 convolution_convert_fusion
  19.5 0.0 all-gather.7.cloned.1.call-update
  19.5 0.0 reduce-scatter.2.cloned.1.call-start
  19.5 0.1 fusion.25
  20.3 1.1 fusion.26
  21.5 0.7 select_reduce_fusion
  22.2 0.1 iota_add_fusion
  22.3 0.1 add.141
  22.4 0.1 convert_reduce_fusion
  22.5 1.4 compare_and_fusion
  23.9 0.5 fusion.8
  24.4 0.5 convolution_bitcast_fusion.1
  24.9 0.2 fusion.29
  25.2 1.2 reshape.261
  26.4 0.6 dynamic-slice
  27.6 0.2 dynamic-update-slice
  27.9 12.6 %all-reduce = bf16[64]{0:T(256)(128)(2,1)S(1)} all-reduce(bf16[64]{0:T(256)(128)(2,1)S(1)} %dynamic-update-slice), channel_id=2, replica_groups=mesh['ctx'=8,'tp'=4] {'ctx'}, use_global_device_ids=true, to_apply=%add | all-reduce | flops 64 | bytes 256
  40.5 0.1 reshape.271
  40.6 0.1 broadcast_in_dim.109
  40.7 0.1 collective-permute-start.2
  40.8 0.0 collective-permute-done.1
  40.8 2.6 %collective-permute-start.3 = (bf16[4,64,256]{2,1,0:T(8,128)(2,1)}, bf16[4,64,256]{2,1,0:T(8,128)(2,1)S(1)}, u32[]{:S(2)}, u32[]{:S(2)}) collective-permute-start(bf16[4,64,256]{2,1,0:T(8,128)(2,1)} %collective-permute-done.1), channel_id=1, source_target_pairs={{0,28},{4,0},{8,4},{12,8},{16,12},{20,16},{24,20},{28,24},{1,29},{... | collective-permute-start | bytes 393224 | tf_op jit(solution)/shard_map/ppermute | solution.py:139
  43.4 0.9 constant_dynamic-update-slice_fusion.6
  44.4 0.9 constant_dynamic-update-slice_fusion.5
  45.3 2.3 %collective-permute-done.2 = bf16[4,64,256]{2,1,0:T(8,128)(2,1)S(1)} collective-permute-done((bf16[4,64,256]{2,1,0:T(8,128)(2,1)}, bf16[4,64,256]{2,1,0:T(8,128)(2,1)S(1)}, u32[]{:S(2)}, u32[]{:S(2)}) %collective-permute-start.2) | collective-permute-done | bytes 131104 | tf_op jit(solution)/shard_map/ppermute | solution.py:131
  47.6 1.5 collective-permute-done.3
  49.1 2.7 %collective-permute-start.5 = (bf16[4,64,256]{2,1,0:T(8,128)(2,1)S(1)}, bf16[4,64,256]{2,1,0:T(8,128)(2,1)S(1)}, u32[]{:S(2)}, u32[]{:S(2)}) collective-permute-start(bf16[4,64,256]{2,1,0:T(8,128)(2,1)S(1)} %collective-permute-done.3), channel_id=1, source_target_pairs={{0,28},{4,0},{8,4},{12,8},{16,12},{20,16},{24,20},{28,24},{1,29},{... | collective-permute-start | bytes 393224 | tf_op jit(solution)/shard_map/ppermute | solution.py:139
  51.9 2.2 %collective-permute-done.4 = bf16[4,64,256]{2,1,0:T(8,128)(2,1)S(1)} collective-permute-done((bf16[4,64,256]{2,1,0:T(8,128)(2,1)S(1)}, bf16[4,64,256]{2,1,0:T(8,128)(2,1)S(1)}, u32[]{:S(2)}, u32[]{:S(2)}) %collective-permute-start.4) | collective-permute-done | bytes 131104 | tf_op jit(solution)/shard_map/ppermute | solution.py:131
  54.1 0.0 collective-permute-start.6
  54.1 1.4 collective-permute-done.5
  55.6 3.8 %collective-permute-done.6 = bf16[4,64,256]{2,1,0:T(8,128)(2,1)S(1)} collective-permute-done((bf16[4,64,256]{2,1,0:T(8,128)(2,1)S(1)}, bf16[4,64,256]{2,1,0:T(8,128)(2,1)S(1)}, u32[]{:S(2)}, u32[]{:S(2)}) %collective-permute-start.6) | collective-permute-done | bytes 131104 | tf_op jit(solution)/shard_map/ppermute | solution.py:131
  59.4 1.1 reshape.258
  60.5 1.3 reshape.260
  61.9 8.3 %fusion = (f32[256,2,4]{0,2,1:T(4,128)S(1)}, f32[2,2048,256,4]{2,1,3,0:T(8,128)}) fusion(pred[256,2048]{0,1:T(8,128)(4,1)S(1)} %compare_and_fusion, bf16[256,2,4,128]{3,2,1,0:T(4,128)(2,1)} %reshape.261, bf16[2048,2,128,1]{2,1,0,3:T(2,128)(2,1)S(1)} %bitcast.103), kind=kOutput, calls=%fused_computation.4 | convolution fusion | flops 1086322688 | bytes 18882560 | tf_op jit(solution)/shard_map/tgjd,sgd->tgjs/dot_general | solution.py:147
  70.2 9.3 %fusion.3 = f32[256,2,4]{0,2,1:T(4,128)S(1)} fusion(f32[2,2048,256,4]{2,1,3,0:T(8,128)} %get-tuple-element.65, f32[256,2,4]{0,2,1:T(4,128)S(1)} %broadcast_maximum_fusion, pred[256,2048]{0,1:T(8,128)(4,1)S(1)} %compare_and_fusion), kind=kLoop, calls=%fused_computation.7 | loop fusion | flops 16775168 | bytes 17317888 | tf_op jit(solution)/shard_map/reduce_sum | solution.py:153
  79.5 7.7 %divide_convert_fusion = bf16[256,2,4,128]{0,3,2,1:T(8,128)(2,1)S(1)} fusion(f32[2,2048,256,4]{2,1,3,0:T(8,128)} %get-tuple-element.65, f32[256,2,4]{0,2,1:T(4,128)S(1)} %broadcast_maximum_fusion, pred[256,2048]{0,1:T(8,128)(4,1)S(1)} %compare_and_fusion, bf16[2048,2,128,1]{2,1,0,3:T(2,128)(2,1)S(1)} %bitcast.102, f32[256,2,4]{0,2,1:T(4,128)S(1)} %fusion.3), kind=kOutput, calls=%fused_computation.28 | convolution fusion | flops 1091043328 | bytes 18890752 | tf_op jit(solution)/shard_map/tgjs,sgd->tgjd/dot_general | solution.py:155
  87.2 0.0 copy-start.4
  87.2 7.7 %fusion.33 = f32[256,4096]{1,0:T(8,128)} fusion(bf16[256,1024]{0,1:T(8,128)(2,1)S(1)} %bitcast.105, bf16[1024,4096]{1,0:T(8,128)(2,1)} %param.24), kind=kOutput, calls=%fused_computation.65 | convolution fusion | flops 2147483648 | bytes 13107200 | tf_op jit(solution)/shard_map/dot_general | solution.py:191
  94.9 0.2 while.12
  95.1 0.1 broadcast_in_dim.124
  95.2 0.7 fusion.15
  96.0 8.9 %convolution_add_fusion = f32[256,4096]{1,0:T(8,128)} fusion(f32[256,4096]{1,0:T(8,128)} %fusion.33, bf16[256,1024]{0,1:T(8,128)(2,1)S(1)} %bitcast.101, bf16[1024,4096]{1,0:T(8,128)(2,1)} %param.25), kind=kOutput, calls=%fused_computation.11 | convolution fusion | flops 2148532224 | bytes 17301504 | tf_op jit(solution)/shard_map/dot_general | solution.py:192
  104.9 0.0 reduce-scatter.2.cloned.1.call-update
  104.9 83.0 %reduce-scatter.2.cloned.1.call-done = f32[64,4096]{1,0:T(8,128)} async-done(((f32[256,4096]{1,0:T(8,128)}), f32[64,4096]{1,0:T(8,128)}) %reduce-scatter.2.cloned.1.call-update) | async-done | bytes 1048592 | tf_op jit(solution)/shard_map/reduce_scatter | solution.py:190
  187.9 2.1 %convert_element_type.103 = bf16[64,4096]{1,0:T(8,128)(2,1)} convert(f32[64,4096]{1,0:T(8,128)} %reduce-scatter.2.cloned.1.call-done) | non-fusion elementwise | flops 262144 | bytes 1572864 | tf_op jit(solution)/shard_map/convert_element_type | solution.py:197
  (29 shorter events, 0.2 us)
Async XLA Ops:
  6.5 13.8 %copy-start = (bf16[256,256]{1,0:T(8,128)(2,1)S(1)}, bf16[256,256]{1,0:T(8,128)(2,1)}, u32[]{:S(2)}) copy-start(bf16[256,256]{1,0:T(8,128)(2,1)} %param.19) | copy-start | bytes 393220
  6.5 19.9 %copy-start.5 = (u32[32]{0:T(128)S(1)}, u32[32]{0:T(128)}, u32[]{:S(2)}) copy-start(u32[32]{0:T(128)} %constant.107) | copy-start | bytes 388
  6.5 34.2 %copy-start.3 = (bf16[4,64,256]{2,1,0:T(8,128)(2,1)S(1)}, bf16[4,64,256]{2,1,0:T(8,128)(2,1)}, u32[]{:S(2)}) copy-start(bf16[4,64,256]{2,1,0:T(8,128)(2,1)} %param.16) | copy-start | bytes 393220
  6.5 18.7 %copy-start.2 = (bf16[256,1024]{1,0:T(8,128)(2,1)S(1)}, bf16[256,1024]{1,0:T(8,128)(2,1)}, u32[]{:S(2)}) copy-start(bf16[256,1024]{1,0:T(8,128)(2,1)} %param.14) | copy-start | bytes 1572868
  6.5 54.0 %all-gather.5.cloned.1.call-start = ((), (), s32[]{:S(2)}) async-start(), calls=%async_computation.1 | async-start | bytes 1179648 | tf_op jit(solution)/shard_map/all_gather | solution.py:110
  7.3 87.6 %all-gather.7.cloned.1.call-start = ((), (), s32[]{:S(2)}) async-start(), calls=%async_computation.3 | async-start | bytes 2359296 | tf_op jit(solution)/shard_map/all_gather | solution.py:14
  7.3 33.4 %collective-permute-start = (bf16[4,64,256]{2,1,0:T(8,128)(2,1)}, bf16[4,64,256]{2,1,0:T(8,128)(2,1)}, u32[]{:S(2)}, u32[]{:S(2)}) collective-permute-start(bf16[4,64,256]{2,1,0:T(8,128)(2,1)} %param.16), channel_id=1, source_target_pairs={{0,4},{4,8},{8,12},{12,16},{16,20},{20,24},{24,28},{28,0},{1,5},{5... | collective-permute-start | bytes 393224 | tf_op jit(solution)/shard_map/ppermute | solution.py:131
  7.8 33.0 %collective-permute-start.1 = (bf16[4,64,256]{2,1,0:T(8,128)(2,1)}, bf16[4,64,256]{2,1,0:T(8,128)(2,1)}, u32[]{:S(2)}, u32[]{:S(2)}) collective-permute-start(bf16[4,64,256]{2,1,0:T(8,128)(2,1)} %param.16), channel_id=1, source_target_pairs={{0,28},{4,0},{8,4},{12,8},{16,12},{20,16},{24,20},{28,24},{1,29},{... | collective-permute-start | bytes 393224 | tf_op jit(solution)/shard_map/ppermute | solution.py:139
  19.5 168.5 %reduce-scatter.2.cloned.1.call-start = ((), (), s32[]{:S(2)}) async-start(), calls=%async_computation.2 | async-start | bytes 5242880 | tf_op jit(solution)/shard_map/reduce_scatter | solution.py:190
  40.7 6.9 %collective-permute-start.2 = (bf16[4,64,256]{2,1,0:T(8,128)(2,1)}, bf16[4,64,256]{2,1,0:T(8,128)(2,1)S(1)}, u32[]{:S(2)}, u32[]{:S(2)}) collective-permute-start(bf16[4,64,256]{2,1,0:T(8,128)(2,1)} %collective-permute-done), channel_id=1, source_target_pairs={{0,4},{4,8},{8,12},{12,16},{16,20},{20,24},{24,28},{28,0},{1,5},{5... | collective-permute-start | bytes 393224 | tf_op jit(solution)/shard_map/ppermute | solution.py:131
  40.8 8.3 %collective-permute-start.3 = (bf16[4,64,256]{2,1,0:T(8,128)(2,1)}, bf16[4,64,256]{2,1,0:T(8,128)(2,1)S(1)}, u32[]{:S(2)}, u32[]{:S(2)}) collective-permute-start(bf16[4,64,256]{2,1,0:T(8,128)(2,1)} %collective-permute-done.1), channel_id=1, source_target_pairs={{0,28},{4,0},{8,4},{12,8},{16,12},{20,16},{24,20},{28,24},{1,29},{... | collective-permute-start | bytes 393224 | tf_op jit(solution)/shard_map/ppermute | solution.py:139
  47.6 6.5 %collective-permute-start.4 = (bf16[4,64,256]{2,1,0:T(8,128)(2,1)S(1)}, bf16[4,64,256]{2,1,0:T(8,128)(2,1)S(1)}, u32[]{:S(2)}, u32[]{:S(2)}) collective-permute-start(bf16[4,64,256]{2,1,0:T(8,128)(2,1)S(1)} %collective-permute-done.2), channel_id=1, source_target_pairs={{0,4},{4,8},{8,12},{12,16},{16,20},{20,24},{24,28},{28,0},{1,5},{5... | collective-permute-start | bytes 393224 | tf_op jit(solution)/shard_map/ppermute | solution.py:131
  49.1 6.4 %collective-permute-start.5 = (bf16[4,64,256]{2,1,0:T(8,128)(2,1)S(1)}, bf16[4,64,256]{2,1,0:T(8,128)(2,1)S(1)}, u32[]{:S(2)}, u32[]{:S(2)}) collective-permute-start(bf16[4,64,256]{2,1,0:T(8,128)(2,1)S(1)} %collective-permute-done.3), channel_id=1, source_target_pairs={{0,28},{4,0},{8,4},{12,8},{16,12},{20,16},{24,20},{28,24},{1,29},{... | collective-permute-start | bytes 393224 | tf_op jit(solution)/shard_map/ppermute | solution.py:139
  54.1 5.3 %collective-permute-start.6 = (bf16[4,64,256]{2,1,0:T(8,128)(2,1)S(1)}, bf16[4,64,256]{2,1,0:T(8,128)(2,1)S(1)}, u32[]{:S(2)}, u32[]{:S(2)}) collective-permute-start(bf16[4,64,256]{2,1,0:T(8,128)(2,1)S(1)} %collective-permute-done.4), channel_id=1, source_target_pairs={{0,4},{4,8},{8,12},{12,16},{16,20},{20,24},{24,28},{28,0},{1,5},{5... | collective-permute-start | bytes 393224 | tf_op jit(solution)/shard_map/ppermute | solution.py:131
  70.2 9.3 %copy-start.1 = (bf16[2048,2,128]{2,1,0:T(2,128)(2,1)S(1)}, bf16[2048,2,128]{2,1,0:T(2,128)(2,1)}, u32[]{:S(2)}) copy-start(bf16[2048,2,128]{2,1,0:T(2,128)(2,1)} %reshape.258) | copy-start | bytes 3145732
  87.2 8.1 %copy-start.4 = (f32[8]{0:T(128)S(1)}, f32[8]{0:T(128)}, u32[]{:S(2)}) copy-start(f32[8]{0:T(128)} %param.21) | copy-start | bytes 100
Sparse Core Ops, SparseCore 0:
  9.3 26.2 all-gather.4
  37.5 30.0 all-gather.6
  105.0 82.8 reduce-scatter.1
